TPU v7x, 256 devices: a whole 4x4x8 slice. The times are simulated.
256 devices in a mesh: pair: 32 (over x, z_hi, y), rows: 8 (over z_lo, core).
Axes of the slice: x: 4, y: 4, z: 8 (z_hi: 2, z_lo: 4; z = z_hi * 4 + z_lo), core: 2. Of those that a mesh axis runs over, the one named last changes fastest.
Arguments:
- samples: float32 [32768, 4096], P(('pair', 'rows')), may hold values from -400 to 400
- keep_mask: int32 [256, 8], P(('pair', 'rows')), may hold values 0 or 1
- keep_rate: float32 [8], replicated, may hold values from 0.5 to 1
Outputs:
- cosine: float32 [64, 512, 512], P('pair', 'rows')
All inputs are finite; a program needn't handle non-finite values. No bound on the sum of `keep_mask` on one device may be relied on, other than what follows from the above.
Results may differ from a plain program's by a relative error of at most 0.00005.
Values sent between devices are 32-bit elements; how exact they have to be, the bound alone decides.
A program may use at most 128 MiB of HBM per device.

v0:
```python
import jax
import jax.numpy as jnp
from jax import lax
from jax.sharding import Mesh
from jax.sharding import PartitionSpec as P

BLOCKS = 8
BLOCK_COLS = 512
BLOCK_ROWS = 128
COLS = 4096
PAIR = ("pair_0", "pair_1", "pair_2")
ROWS = ("rows_0", "rows_1")
PAIR_ROWS = ("pair_0", "pair_1", "pair_2", "rows_0", "rows_1")
EPS = 1e-06


def one_axis_at_a_time(value, axes):
    for axis in axes:
        value = lax.psum(value, axis)
    return value


def reduced_to_own(tiles, axes, turns):
    inside = tiles.shape[1:]
    tiles = tiles.reshape(*(lax.axis_size(a) for a in axes), *inside)
    tiles = jnp.moveaxis(tiles, turns, range(len(axes))).reshape(-1, *inside)
    for k in turns:
        tiles = lax.psum_scatter(tiles, axes[k], scatter_dimension=0, tiled=True)
    return tiles[0]


def in_blocks(value, dim, count):
    lengths = value.shape
    tiles = value.reshape(*lengths[:dim], count, lengths[dim] // count, *lengths[dim + 1 :])
    return jnp.moveaxis(tiles, dim, 0)


def scatter_axes(value, axes, turns, dim):
    count = lax.axis_size(axes)
    return reduced_to_own(in_blocks(value, dim, count), axes, turns)


def per_device(samples, keep_mask, keep_rate):
    pair_count = lax.axis_size(PAIR)
    row_count = lax.axis_size(ROWS)
    tile_count = BLOCKS * BLOCKS // pair_count
    pair_index = lax.axis_index(PAIR)
    row_index = lax.axis_index(ROWS)
    local_rows = samples.shape[0]
    slice_rows = BLOCK_COLS // row_count
    squares = jnp.sum(samples * samples, axis=0)
    col_norms = jnp.sqrt(one_axis_at_a_time(squares, PAIR_ROWS) + EPS)
    weights = keep_mask.astype(jnp.float32)
    masked = (
        samples.reshape(local_rows // BLOCK_ROWS, BLOCK_ROWS, BLOCKS, BLOCK_COLS)
        * weights[:, None, :, None]
    )
    masked_rows = masked.reshape(local_rows, COLS)
    initial = jnp.zeros((BLOCKS * BLOCKS, slice_rows, BLOCK_COLS), jnp.float32)
    piece = lax.all_gather(masked_rows, ROWS, axis=0, tiled=True)
    count = piece.shape[0]
    split_cols = piece.reshape(count, BLOCKS, row_count, slice_rows)
    left_cols = lax.dynamic_slice_in_dim(split_cols, row_index, 1, 2)[:, :, 0, :]
    right_cols = piece.reshape(count, BLOCKS, BLOCK_COLS)
    product = jnp.einsum(
        "rai,rbj->abij",
        left_cols,
        right_cols,
        precision=lax.Precision.HIGHEST,
        preferred_element_type=jnp.float32,
    )
    tile_grams = product.reshape(initial.shape)
    summed = scatter_axes(tile_grams, PAIR, (0, 2, 1), 0)
    first_tile = pair_index * tile_count
    left_block = first_tile // BLOCKS
    right_start = first_tile % BLOCKS
    norm_blocks = col_norms.reshape(BLOCKS, BLOCK_COLS)
    row_norms = lax.dynamic_slice(
        norm_blocks, (left_block, row_index * slice_rows), (1, slice_rows)
    )[0]
    col_part = lax.dynamic_slice(norm_blocks, (right_start, jnp.int32(0)), (tile_count, BLOCK_COLS))
    left_rate = lax.dynamic_slice(keep_rate, (left_block,), (1,))
    right_rate = lax.dynamic_slice(keep_rate, (right_start,), (tile_count,))
    row_scale = left_rate * row_norms
    col_scale = right_rate[:, None] * col_part
    return summed / (row_scale[None, :, None] * col_scale[:, None, :])


def solution(mesh):
    finer = Mesh(
        mesh.devices.reshape(4, 2, 4, 4, 2), ("pair_0", "pair_1", "pair_2", "rows_0", "rows_1")
    )
    placed = (P(PAIR_ROWS, None), P(PAIR_ROWS, None), P())
    return jax.shard_map(
        per_device, mesh=finer, in_specs=placed, out_specs=P(PAIR, ROWS, None), check_vma=False
    )
```

profile of v0, /device:TPU:1, one launch (start us, length us, event | category | flops | bytes accessed | tf_op | source)
XLA Modules:
  0.0 418.9 jit_solution(9704003310913359644)
XLA Ops:
  6.5 0.0 copy-start.1
  6.5 0.0 all-gather.2.cloned.1.call-start
  6.5 1.9 copy.6
  8.5 0.0 copy-done.1
  8.5 0.1 broadcast_bitcast_fusion
  8.6 2.0 broadcast_multiply_fusion
  10.5 0.0 all-gather.2.cloned.1.call-update
  10.6 0.0 reduce-scatter.4.cloned.1.call-start
  10.6 175.9 %all-gather.2.cloned.1.call-done = f32[1024,4096]{0,1:T(8,128)} async-done(((f32[128,4096]{0,1:T(8,128)}), f32[1024,4096]{0,1:T(8,128)}) %all-gather.2.cloned.1.call-update) | async-done | bytes 16777232 | tf_op jit(solution)/shard_map/all_gather | solution.py:60
  186.5 30.1 %fusion = f32[8,512,8,64]{1,3,2,0:T(8,128)S(1)} fusion(f32[1024,8,512,1]{0,2,3,1:T(8,128)} %bitcast.30, f32[1024,8,8,64]{0,3,2,1:T(8,128)} %bitcast.31, s32[]{:T(128)S(6)} %select_n.25), kind=kOutput, calls=%fused_computation | convolution fusion | flops 25769803776 | bytes 27262980 | tf_op jit(solution)/shard_map/rai,rbj->abij/dot_general | solution.py:65
  216.6 4.3 %copy.8 = f32[4,4,2,2,64,512]{5,4,3,2,1,0:T(8,128)} copy(f32[4,4,2,2,64,512]{5,4,2,0,3,1:T(8,128)S(1)} %bitcast.28) | data formatting | bytes 16777216 | tf_op jit(solution)/shard_map/transpose | solution.py:26
  220.9 0.0 reduce-scatter.4.cloned.1.call-update
  220.9 0.0 copy-start
  221.0 0.0 reduce-scatter.6.cloned.1.call-start
  221.0 82.4 %reduce-scatter.4.cloned.1.call-done = f32[8,2,64,512]{3,2,1,0:T(8,128)} async-done(((f32[32,2,64,512]{3,2,1,0:T(8,128)}), f32[8,2,64,512]{3,2,1,0:T(8,128)}) %reduce-scatter.4.cloned.1.call-update) | async-done | bytes 2097168 | tf_op jit(solution)/shard_map/reduce_scatter | solution.py:28
  303.4 0.0 reduce-scatter.6.cloned.1.call-update
  303.5 0.0 reduce-scatter.8.cloned.1.call-start
  303.5 34.6 %reduce-scatter.6.cloned.1.call-done = f32[2,2,64,512]{3,2,1,0:T(8,128)} async-done(((f32[8,2,64,512]{3,2,1,0:T(8,128)}), f32[2,2,64,512]{3,2,1,0:T(8,128)}) %reduce-scatter.6.cloned.1.call-update) | async-done | bytes 524304 | tf_op jit(solution)/shard_map/reduce_scatter | solution.py:28
  338.1 0.0 reduce-scatter.8.cloned.1.call-update
  338.2 0.0 copy-done
  338.2 0.2 multiply_reduce_fusion
  338.3 13.1 %psum.35 = f32[4096]{0:T(1024)S(1)} all-reduce(f32[4096]{0:T(1024)S(1)} %multiply_reduce_fusion), channel_id=1, replica_groups=mesh['pair_0'=4,'pair_1'=2,'pair_2'=4,'rows_0'=4,'rows_1'=2] {'pair_0'}, use_global_device_ids=true, to_apply=%region_4.0 | all-reduce | flops 4096 | bytes 32768 | tf_op jit(solution)/shard_map/psum | solution.py:19
  351.4 18.0 %psum.36 = f32[4096]{0:T(1024)S(1)} all-reduce(f32[4096]{0:T(1024)S(1)} %psum.35), channel_id=1, replica_groups=mesh['pair_0'=4,'pair_1'=2,'pair_2'=4,'rows_0'=4,'rows_1'=2] {'pair_1'}, use_global_device_ids=true, to_apply=%region_5.0 | all-reduce | flops 4096 | bytes 32768 | tf_op jit(solution)/shard_map/psum | solution.py:19
  369.4 12.0 %psum.37 = f32[4096]{0:T(1024)S(1)} all-reduce(f32[4096]{0:T(1024)S(1)} %psum.36), channel_id=1, replica_groups=mesh['pair_0'=4,'pair_1'=2,'pair_2'=4,'rows_0'=4,'rows_1'=2] {'pair_2'}, use_global_device_ids=true, to_apply=%region_6.0 | all-reduce | flops 4096 | bytes 32768 | tf_op jit(solution)/shard_map/psum | solution.py:19
  381.4 12.4 %psum.38 = f32[4096]{0:T(1024)S(1)} all-reduce(f32[4096]{0:T(1024)S(1)} %psum.37), channel_id=1, replica_groups=mesh['pair_0'=4,'pair_1'=2,'pair_2'=4,'rows_0'=4,'rows_1'=2] {'rows_0'}, use_global_device_ids=true, to_apply=%region_7.0 | all-reduce | flops 4096 | bytes 32768 | tf_op jit(solution)/shard_map/psum | solution.py:19
  393.8 15.3 %psum.39 = f32[4096]{0:T(1024)S(1)} all-reduce(f32[4096]{0:T(1024)S(1)} %psum.38), channel_id=1, replica_groups=mesh['pair_0'=4,'pair_1'=2,'pair_2'=4,'rows_0'=4,'rows_1'=2] {'rows_1'}, use_global_device_ids=true, to_apply=%region_8.0 | all-reduce | flops 4096 | bytes 32768 | tf_op jit(solution)/shard_map/psum | solution.py:19
  409.2 0.0 copy-done.2
  409.2 0.1 dynamic_slice.18
  409.3 0.6 dynamic_slice.16
  409.8 0.7 multiply_bitcast_fusion
  410.6 0.1 dynamic-slice_multiply_fusion
  410.6 1.8 bitcast_divide_fusion
  (6 shorter events, 0.0 us)
Async XLA Ops:
  6.5 1.9 copy-start.1
  6.5 180.0 %all-gather.2.cloned.1.call-start = ((), (), s32[]{:S(2)}) async-start(), calls=%async_computation.3 | async-start | bytes 18874368 | tf_op jit(solution)/shard_map/all_gather | solution.py:60
  10.6 292.9 %reduce-scatter.4.cloned.1.call-start = ((), (), s32[]{:S(2)}) async-start(), calls=%async_computation.4 | async-start | bytes 10485760 | tf_op jit(solution)/shard_map/reduce_scatter | solution.py:28
  220.9 117.2 %copy-start = (f32[128,4096]{1,0:T(8,128)S(1)}, f32[128,4096]{1,0:T(8,128)}, u32[]{:S(2)}) copy-start(f32[128,4096]{1,0:T(8,128)} %param.3) | copy-start | bytes 6291460
  221.0 117.1 %reduce-scatter.6.cloned.1.call-start = ((), (), s32[]{:S(2)}) async-start(), calls=%async_computation.5 | async-start | bytes 2621440 | tf_op jit(solution)/shard_map/reduce_scatter | solution.py:28
  303.4 105.7 %copy-start.2 = (f32[8]{0:T(128)S(1)}, f32[8]{0:T(128)}, u32[]{:S(2)}) copy-start(f32[8]{0:T(128)} %param.5) | copy-start | bytes 100
  303.5 107.2 %reduce-scatter.8.cloned.1.call-start = ((), (), s32[]{:S(2)}) async-start(), calls=%async_computation.6 | async-start | bytes 786432 | tf_op jit(solution)/shard_map/reduce_scatter | solution.py:28
Sparse Core Ops, SparseCore 0:
  10.7 175.8 all-gather.1
  221.1 82.3 reduce-scatter.3
  306.0 32.0 reduce-scatter.5
  340.4 29.7 reduce-scatter.7
where the time goes:
time: 419 us
  waiting for transfers between devices  293 us (70%)
  blocking collectives  70.8 us (17%)
  matrix products  30.1 us (7%)
  between operations  13.2 us (3%)
  local copies, waits for them, and re-layouts  6.96 us (2%)
  other arithmetic  4.7 us (1%)
    all_gather x1, waiting for transfers between devices, per_device(): piece = lax.all_gather(masked_rows, ROWS, axis=0, tiled=True)  176 us
    reduce_scatter x3, waiting for transfers between devices, reduced_to_own(): tiles = lax.psum_scatter(tiles, axes[k], scatter_dimension=0, tiled=True)  117 us
    psum x5, blocking collectives, one_axis_at_a_time(): value = lax.psum(value, axis)  70.8 us
    dot_general x1, matrix products, per_device(): jnp.einsum('rai,rbj->abij', left_cols, right_cols, precision=lax.Precisio...  30.1 us
  transfers between devices with their start and end apart: 4, of which 3 were waited for; matrix products, arithmetic and copies ran while one was open for 0% of the time, Pallas kernels for 0%

commit v1 on v0

--- a/solution.py
+++ b/solution.py
@@ -57,7 +57,9 @@
     )
     masked_rows = masked.reshape(local_rows, COLS)
     initial = jnp.zeros((BLOCKS * BLOCKS, slice_rows, BLOCK_COLS), jnp.float32)
-    piece = lax.all_gather(masked_rows, ROWS, axis=0, tiled=True)
+    piece = jnp.concatenate(
+        lax.all_to_all(jnp.stack([masked_rows] * lax.axis_size(ROWS)), ROWS, 0, 0), axis=0
+    )
     count = piece.shape[0]
     split_cols = piece.reshape(count, BLOCKS, row_count, slice_rows)
     left_cols = lax.dynamic_slice_in_dim(split_cols, row_index, 1, 2)[:, :, 0, :]

time: 419 us -> 704 us (1.68)
  waiting for transfers between devices: 293 us -> 482 us
  local copies, waits for them, and re-layouts: 6.96 us -> 87.9 us
  starting transfers between devices: 0.12 us -> 8.91 us
    all_to_all x0 -> x1, waiting for transfers between devices: none -> 363 us  [per_device(): lax.all_to_all(jnp.stack([masked_rows] * lax.axis_size(ROWS)), ROWS, 0, 0)]
    all_gather x1 -> x0, waiting for transfers between devices: 176 us -> none  [per_device(): piece = lax.all_gather(masked_rows, ROWS, axis=0, tiled=True)]
    all_to_all x0 -> x2, local copies, waits for them, and re-layouts: none -> 35.2 us  [per_device(): lax.all_to_all(jnp.stack([masked_rows] * lax.axis_size(ROWS)), ROWS, 0, 0)]
    another operation x0 -> x2, local copies, waits for them, and re-layouts: none -> 24.8 us  [the longest x1 18 us: per_device(): split_cols = piece.reshape(count, BLOCKS, row_count, slice_rows)]
    unnamed x9 -> x5, local copies, waits for them, and re-layouts: 2.01 us -> 21.1 us
    all_to_all x0 -> x1, starting transfers between devices: none -> 8.83 us  [per_device(): lax.all_to_all(jnp.stack([masked_rows] * lax.axis_size(ROWS)), ROWS, 0, 0)]
where the time goes in v1:
time: 704 us; the launch traced here: 703 us
  waiting for transfers between devices  482 us (68%)
  local copies, waits for them, and re-layouts  87.9 us (12%)
  blocking collectives  70.6 us (10%)
  matrix products  33.9 us (5%)
  between operations  13.2 us (2%)
  starting transfers between devices  8.91 us (1%)
    all_to_all x1, waiting for transfers between devices, per_device(): lax.all_to_all(jnp.stack([masked_rows] * lax.axis_size(ROWS)), ROWS, 0, 0)  363 us
    reduce_scatter x3, waiting for transfers between devices, reduced_to_own(): tiles = lax.psum_scatter(tiles, axes[k], scatter_dimension=0, tiled=True)  119 us
    psum x5, blocking collectives, one_axis_at_a_time(): value = lax.psum(value, axis)  70.6 us
    all_to_all x2, local copies, waits for them, and re-layouts, per_device(): lax.all_to_all(jnp.stack([masked_rows] * lax.axis_size(ROWS)), ROWS, 0, 0)  35.2 us
    dot_general x1, matrix products, per_device(): jnp.einsum('rai,rbj->abij', left_cols, right_cols, precision=lax.Precisio...  33.9 us
    unnamed x5, local copies, waits for them, and re-layouts  21.1 us
    another operation x1, local copies, waits for them, and re-layouts, per_device(): split_cols = piece.reshape(count, BLOCKS, row_count, slice_rows)  18 us
  transfers between devices with their start and end apart: 4, of which 3 were waited for; matrix products, arithmetic and copies ran while one was open for 0% of the time, Pallas kernels for 0%

profile of v1, /device:TPU:1, one launch (start us, length us, event | category | flops | bytes accessed | tf_op | source)
XLA Modules:
  0.0 703.0 jit_solution(9471174515130418064)
XLA Ops:
  6.5 0.7 convert_bitcast_fusion
  7.2 0.1 broadcast_bitcast_fusion
  7.3 3.2 multiply_reduce_fusion
  10.5 1.9 copy.9
  12.4 6.8 stack.3
  19.2 8.8 %all-to-all-start = ((f32[8,128,4096]{1,2,0:T(8,128)}), f32[8,128,4096]{1,2,0:T(8,128)}, u32[]{:S(2)}, u32[]{:S(2)}) async-start(f32[8,128,4096]{1,2,0:T(8,128)} %stack.3), calls=%async_computation | async-start | bytes 33554432 | tf_op jit(solution)/shard_map/all_to_all | solution.py:61
  28.0 0.0 reduce-scatter.4.cloned.1.call-start
  28.0 362.8 %all-to-all-done = f32[8,128,4096]{1,2,0:T(8,128)} async-done(((f32[8,128,4096]{1,2,0:T(8,128)}), f32[8,128,4096]{1,2,0:T(8,128)}, u32[]{:S(2)}, u32[]{:S(2)}) %all-to-all-start) | async-done | bytes 16777248 | tf_op jit(solution)/shard_map/all_to_all | solution.py:61
  390.8 17.5 %copy.10 = f32[8,128,4096]{2,1,0:T(8,128)} copy(f32[8,128,4096]{1,2,0:T(8,128)} %all-to-all-done) | data formatting | bytes 33554432 | tf_op jit(solution)/shard_map/all_to_all | solution.py:61
  408.3 21.0 %copy.18 = f32[128,8,8,512]{3,2,1,0:T(8,128)} copy(f32[128,8,8,512]{3,1,2,0:T(8,128)} %bitcast.27) | data formatting | bytes 33554432
  429.3 17.7 %copy.11 = f32[8,128,4096]{1,0,2:T(8,128)} copy(f32[8,128,4096]{1,2,0:T(8,128)} %all-to-all-done) | data formatting | bytes 33554432 | tf_op jit(solution)/shard_map/all_to_all | solution.py:61
  447.0 18.0 %reshape_reshape.7 = f32[1024,8,8,64]{0,3,2,1:T(8,128)} reshape(f32[8,128,4096]{1,0,2:T(8,128)} %copy.11) | data formatting | bytes 33554432 | tf_op jit(solution)/shard_map/reshape;reshape | solution.py:64
  465.0 33.9 %fusion = f32[8,512,8,64]{1,3,2,0:T(8,128)S(1)} fusion(f32[1024,8,512,1]{2,1,0,3:T(8,128)} %bitcast.29, f32[1024,8,8,64]{0,3,2,1:T(8,128)} %reshape_reshape.7, s32[]{:T(128)S(6)} %select_n.25), kind=kOutput, calls=%fused_computation | convolution fusion | flops 25769803776 | bytes 27262980 | tf_op jit(solution)/shard_map/rai,rbj->abij/dot_general | solution.py:67
  498.9 4.3 copy.13
  503.2 0.0 reduce-scatter.4.cloned.1.call-update
  503.2 0.0 reduce-scatter.6.cloned.1.call-start
  503.2 84.7 %reduce-scatter.4.cloned.1.call-done = f32[8,2,64,512]{3,2,1,0:T(8,128)} async-done(((f32[32,2,64,512]{3,2,1,0:T(8,128)}), f32[8,2,64,512]{3,2,1,0:T(8,128)}) %reduce-scatter.4.cloned.1.call-update) | async-done | bytes 2097168 | tf_op jit(solution)/shard_map/reduce_scatter | solution.py:28
  587.9 0.0 reduce-scatter.6.cloned.1.call-update
  587.9 0.0 reduce-scatter.8.cloned.1.call-start
  588.0 34.5 %reduce-scatter.6.cloned.1.call-done = f32[2,2,64,512]{3,2,1,0:T(8,128)} async-done(((f32[8,2,64,512]{3,2,1,0:T(8,128)}), f32[2,2,64,512]{3,2,1,0:T(8,128)}) %reduce-scatter.6.cloned.1.call-update) | async-done | bytes 524304 | tf_op jit(solution)/shard_map/reduce_scatter | solution.py:28
  622.5 0.0 reduce-scatter.8.cloned.1.call-update
  622.6 0.0 copy-done
  622.6 0.6 dynamic_slice.16
  623.2 0.1 dynamic_slice.18
  623.3 13.0 %psum.35 = f32[4096]{0:T(1024)S(1)} all-reduce(f32[4096]{0:T(1024)S(1)} %get-tuple-element.5), channel_id=1, replica_groups=mesh['pair_0'=4,'pair_1'=2,'pair_2'=4,'rows_0'=4,'rows_1'=2] {'pair_0'}, use_global_device_ids=true, to_apply=%region_4.0 | all-reduce | flops 4096 | bytes 32768 | tf_op jit(solution)/shard_map/psum | solution.py:19
  636.3 17.6 %psum.36 = f32[4096]{0:T(1024)S(1)} all-reduce(f32[4096]{0:T(1024)S(1)} %psum.35), channel_id=1, replica_groups=mesh['pair_0'=4,'pair_1'=2,'pair_2'=4,'rows_0'=4,'rows_1'=2] {'pair_1'}, use_global_device_ids=true, to_apply=%region_5.0 | all-reduce | flops 4096 | bytes 32768 | tf_op jit(solution)/shard_map/psum | solution.py:19
  653.9 13.3 %psum.37 = f32[4096]{0:T(1024)S(1)} all-reduce(f32[4096]{0:T(1024)S(1)} %psum.36), channel_id=1, replica_groups=mesh['pair_0'=4,'pair_1'=2,'pair_2'=4,'rows_0'=4,'rows_1'=2] {'pair_2'}, use_global_device_ids=true, to_apply=%region_6.0 | all-reduce | flops 4096 | bytes 32768 | tf_op jit(solution)/shard_map/psum | solution.py:19
  667.2 12.0 %psum.38 = f32[4096]{0:T(1024)S(1)} all-reduce(f32[4096]{0:T(1024)S(1)} %psum.37), channel_id=1, replica_groups=mesh['pair_0'=4,'pair_1'=2,'pair_2'=4,'rows_0'=4,'rows_1'=2] {'rows_0'}, use_global_device_ids=true, to_apply=%region_7.0 | all-reduce | flops 4096 | bytes 32768 | tf_op jit(solution)/shard_map/psum | solution.py:19
  679.2 14.6 %psum.39 = f32[4096]{0:T(1024)S(1)} all-reduce(f32[4096]{0:T(1024)S(1)} %psum.38), channel_id=1, replica_groups=mesh['pair_0'=4,'pair_1'=2,'pair_2'=4,'rows_0'=4,'rows_1'=2] {'rows_1'}, use_global_device_ids=true, to_apply=%region_8.0 | all-reduce | flops 4096 | bytes 32768 | tf_op jit(solution)/shard_map/psum | solution.py:19
  693.9 0.7 multiply_bitcast_fusion
  694.6 0.1 dynamic-slice_multiply_fusion
  694.7 1.8 bitcast_divide_fusion
  (5 shorter events, 0.0 us)
Async XLA Ops:
  19.2 371.6 %all-to-all-start = ((f32[8,128,4096]{1,2,0:T(8,128)}), f32[8,128,4096]{1,2,0:T(8,128)}, u32[]{:S(2)}, u32[]{:S(2)}) async-start(f32[8,128,4096]{1,2,0:T(8,128)} %stack.3), calls=%async_computation | async-start | bytes 33554432 | tf_op jit(solution)/shard_map/all_to_all | solution.py:61
  28.0 559.9 %reduce-scatter.4.cloned.1.call-start = ((), (), s32[]{:S(2)}) async-start(), calls=%async_computation.4 | async-start | bytes 10485760 | tf_op jit(solution)/shard_map/reduce_scatter | solution.py:28
  503.2 119.4 %copy-start = (f32[8]{0:T(128)S(1)}, f32[8]{0:T(128)}, u32[]{:S(2)}) copy-start(f32[8]{0:T(128)} %param.5) | copy-start | bytes 100
  503.2 119.3 %reduce-scatter.6.cloned.1.call-start = ((), (), s32[]{:S(2)}) async-start(), calls=%async_computation.5 | async-start | bytes 2621440 | tf_op jit(solution)/shard_map/reduce_scatter | solution.py:28
  587.9 106.7 %reduce-scatter.8.cloned.1.call-start = ((), (), s32[]{:S(2)}) async-start(), calls=%async_computation.6 | async-start | bytes 786432 | tf_op jit(solution)/shard_map/reduce_scatter | solution.py:28
Sparse Core Ops, SparseCore 0:
  503.3 84.5 reduce-scatter.3
  590.4 32.0 reduce-scatter.5
  625.0 29.7 reduce-scatter.7

commit v2 on v0

--- a/solution.py
+++ b/solution.py
@@ -16,7 +16,7 @@
 
 def one_axis_at_a_time(value, axes):
     for axis in axes:
-        value = lax.psum(value, axis)
+        value = jnp.sum(lax.all_gather(value, axis), axis=0)
     return value
 
 

time: 419 us -> 399 us (0.952)
  blocking collectives: 70.8 us -> 50.2 us
    psum x5 -> x0, blocking collectives: 70.8 us -> none  [one_axis_at_a_time(): value = lax.psum(value, axis)]
    all_gather x0 -> x5, blocking collectives: none -> 50.2 us  [one_axis_at_a_time(): value = jnp.sum(lax.all_gather(value, axis), axis=0)]
where the time goes in v2:
time: 399 us
  waiting for transfers between devices  293 us (73%)
  blocking collectives  50.2 us (13%)
  matrix products  30.1 us (8%)
  between operations  13.3 us (3%)
  local copies, waits for them, and re-layouts  7.08 us (2%)
  other arithmetic  4.9 us (1%)
    all_gather x1, waiting for transfers between devices, per_device(): piece = lax.all_gather(masked_rows, ROWS, axis=0, tiled=True)  176 us
    reduce_scatter x3, waiting for transfers between devices, reduced_to_own(): tiles = lax.psum_scatter(tiles, axes[k], scatter_dimension=0, tiled=True)  117 us
    all_gather x5, blocking collectives, one_axis_at_a_time(): value = jnp.sum(lax.all_gather(value, axis), axis=0)  50.2 us
    dot_general x1, matrix products, per_device(): jnp.einsum('rai,rbj->abij', left_cols, right_cols, precision=lax.Precisio...  30.1 us
  transfers between devices with their start and end apart: 4, of which 3 were waited for; matrix products, arithmetic and copies ran while one was open for 0% of the time, Pallas kernels for 0%

profile of v2, /device:TPU:1, one launch (start us, length us, event | category | flops | bytes accessed | tf_op | source)
XLA Modules:
  0.0 398.8 jit_solution(9222064761971149449)
XLA Ops:
  6.5 0.0 all-gather.7.cloned.1.call-start
  6.5 1.9 copy.12
  8.5 0.0 copy-done.1
  8.5 0.1 broadcast_bitcast_fusion
  8.6 2.0 broadcast_multiply_fusion
  10.5 0.0 all-gather.7.cloned.1.call-update
  10.6 0.0 reduce-scatter.4.cloned.1.call-start
  10.6 175.9 %all-gather.7.cloned.1.call-done = f32[1024,4096]{0,1:T(8,128)} async-done(((f32[128,4096]{0,1:T(8,128)}), f32[1024,4096]{0,1:T(8,128)}) %all-gather.7.cloned.1.call-update) | async-done | bytes 16777232 | tf_op jit(solution)/shard_map/all_gather | solution.py:60
  186.5 30.1 %fusion = f32[8,512,8,64]{1,3,2,0:T(8,128)S(1)} fusion(f32[1024,8,512,1]{0,2,3,1:T(8,128)} %bitcast.30, f32[1024,8,8,64]{0,3,2,1:T(8,128)} %bitcast.31, s32[]{:T(128)S(6)} %select_n.25), kind=kOutput, calls=%fused_computation | convolution fusion | flops 25769803776 | bytes 27262980 | tf_op jit(solution)/shard_map/rai,rbj->abij/dot_general | solution.py:65
  216.6 4.3 %copy.14 = f32[4,4,2,2,64,512]{5,4,3,2,1,0:T(8,128)} copy(f32[4,4,2,2,64,512]{5,4,2,0,3,1:T(8,128)S(1)} %bitcast.28) | data formatting | bytes 16777216 | tf_op jit(solution)/shard_map/transpose | solution.py:26
  220.9 0.0 reduce-scatter.4.cloned.1.call-update
  220.9 0.0 copy-start
  221.0 0.0 reduce-scatter.6.cloned.1.call-start
  221.0 82.4 %reduce-scatter.4.cloned.1.call-done = f32[8,2,64,512]{3,2,1,0:T(8,128)} async-done(((f32[32,2,64,512]{3,2,1,0:T(8,128)}), f32[8,2,64,512]{3,2,1,0:T(8,128)}) %reduce-scatter.4.cloned.1.call-update) | async-done | bytes 2097168 | tf_op jit(solution)/shard_map/reduce_scatter | solution.py:28
  303.4 0.0 reduce-scatter.6.cloned.1.call-update
  303.5 0.0 copy-start.2
  303.5 0.0 reduce-scatter.8.cloned.1.call-start
  303.5 34.6 %reduce-scatter.6.cloned.1.call-done = f32[2,2,64,512]{3,2,1,0:T(8,128)} async-done(((f32[8,2,64,512]{3,2,1,0:T(8,128)}), f32[2,2,64,512]{3,2,1,0:T(8,128)}) %reduce-scatter.6.cloned.1.call-update) | async-done | bytes 524304 | tf_op jit(solution)/shard_map/reduce_scatter | solution.py:28
  338.1 0.0 reduce-scatter.8.cloned.1.call-update
  338.2 0.0 copy-done
  338.2 0.2 multiply_reduce_fusion
  338.3 9.3 %all-gather = f32[16384]{0:T(1024)S(1)} all-gather(f32[4096]{0:T(1024)S(1)} %multiply_reduce_fusion), channel_id=2, replica_groups=mesh['pair_0'=4,'pair_1'=2,'pair_2'=4,'rows_0'=4,'rows_1'=2] {'pair_0'}, dimensions={0}, use_global_device_ids=true | all-gather | bytes 81920 | tf_op jit(solution)/shard_map/all_gather | solution.py:19
  347.7 7.3 %all-gather.1 = f32[8192]{0:T(1024)S(1)} all-gather(f32[4096]{0:T(1024)S(1)} %reduce_sum.55), channel_id=3, replica_groups=mesh['pair_0'=4,'pair_1'=2,'pair_2'=4,'rows_0'=4,'rows_1'=2] {'pair_1'}, dimensions={0}, use_global_device_ids=true | all-gather | bytes 49152 | tf_op jit(solution)/shard_map/all_gather | solution.py:19
  355.0 10.2 %all-gather.2 = f32[16384]{0:T(1024)S(1)} all-gather(f32[4096]{0:T(1024)S(1)} %reduce_sum.56), channel_id=4, replica_groups=mesh['pair_0'=4,'pair_1'=2,'pair_2'=4,'rows_0'=4,'rows_1'=2] {'pair_2'}, dimensions={0}, use_global_device_ids=true | all-gather | bytes 81920 | tf_op jit(solution)/shard_map/all_gather | solution.py:19
  365.3 10.6 %all-gather.3 = f32[16384]{0:T(1024)S(1)} all-gather(f32[4096]{0:T(1024)S(1)} %reduce_sum.57), channel_id=5, replica_groups=mesh['pair_0'=4,'pair_1'=2,'pair_2'=4,'rows_0'=4,'rows_1'=2] {'rows_0'}, dimensions={0}, use_global_device_ids=true | all-gather | bytes 81920 | tf_op jit(solution)/shard_map/all_gather | solution.py:19
  376.0 12.9 %all-gather.4 = f32[8192]{0:T(1024)S(1)} all-gather(f32[4096]{0:T(1024)S(1)} %reduce_sum.58), channel_id=6, replica_groups=mesh['pair_0'=4,'pair_1'=2,'pair_2'=4,'rows_0'=4,'rows_1'=2] {'rows_1'}, dimensions={0}, use_global_device_ids=true | all-gather | bytes 49152 | tf_op jit(solution)/shard_map/all_gather | solution.py:19
  389.0 0.0 copy-done.2
  389.0 0.1 dynamic_slice.18
  389.1 0.6 dynamic_slice.16
  389.7 0.7 multiply_bitcast_fusion
  390.4 0.1 dynamic-slice_multiply_fusion
  390.5 1.8 bitcast_divide_fusion
  (16 shorter events, 0.4 us)
Async XLA Ops:
  6.5 1.9 copy-start.1
  6.5 180.0 %all-gather.7.cloned.1.call-start = ((), (), s32[]{:S(2)}) async-start(), calls=%async_computation.3 | async-start | bytes 18874368 | tf_op jit(solution)/shard_map/all_gather | solution.py:60
  10.6 292.9 %reduce-scatter.4.cloned.1.call-start = ((), (), s32[]{:S(2)}) async-start(), calls=%async_computation.4 | async-start | bytes 10485760 | tf_op jit(solution)/shard_map/reduce_scatter | solution.py:28
  220.9 117.2 %copy-start = (f32[128,4096]{1,0:T(8,128)S(1)}, f32[128,4096]{1,0:T(8,128)}, u32[]{:S(2)}) copy-start(f32[128,4096]{1,0:T(8,128)} %param.3) | copy-start | bytes 6291460
  221.0 117.1 %reduce-scatter.6.cloned.1.call-start = ((), (), s32[]{:S(2)}) async-start(), calls=%async_computation.5 | async-start | bytes 2621440 | tf_op jit(solution)/shard_map/reduce_scatter | solution.py:28
  303.5 85.5 %copy-start.2 = (f32[8]{0:T(128)S(1)}, f32[8]{0:T(128)}, u32[]{:S(2)}) copy-start(f32[8]{0:T(128)} %param.5) | copy-start | bytes 100
  303.5 87.0 %reduce-scatter.8.cloned.1.call-start = ((), (), s32[]{:S(2)}) async-start(), calls=%async_computation.6 | async-start | bytes 786432 | tf_op jit(solution)/shard_map/reduce_scatter | solution.py:28
Sparse Core Ops, SparseCore 0:
  10.7 175.8 all-gather.6
  221.1 82.3 reduce-scatter.3
  306.0 32.0 reduce-scatter.5
  340.4 25.8 reduce-scatter.7
